TPU v7x, 128 devices: a whole 4x4x4 slice. The times are simulated.
128 devices in a mesh: comp: 2 (over core), dom: 64 (over x, y, z).
Axes of the slice: x: 4, y: 4, z: 4, core: 2. Of those that a mesh axis runs over, the one named last changes fastest.
Arguments:
- ocean_state: float32 [4, 80, 65536], P(None, None, ('comp', 'dom')), may hold values from -6 to 6
- atm_flux: float32 [2, 4, 262144], P(None, None, ('comp', 'dom')), may hold values from -6 to 6
- edge_coeff: float32 [7, 65536], P(None, ('comp', 'dom')), may hold values from 0.015 to 0.085
- neighbours: int32 [7, 65536], P(None, ('comp', 'dom')), may hold values from 0 to 1023
- halo_send: int32 [2, 32768], P(None, ('comp', 'dom')), may hold values from 0 to 511
- send_idx: int32 [128, 1024], P(('comp', 'dom')), may hold values from 0 to 2047
- recv_slot: int32 [4, 65536], P(None, ('comp', 'dom')), may hold values from 0 to 1023
- regrid_weight: float32 [4, 65536], P(None, ('comp', 'dom')), may hold values from 0.1 to 1
Outputs:
- final_state: float32 [4, 80, 65536], P(None, None, ('comp', 'dom'))
- atm_surface: float32 [4, 262144], P(None, ('comp', 'dom'))
Inputs may be any that keep to these rules, and one draw needn't show every extreme that they name: `halo_send`: local cell numbers of the sending partition. `neighbours`: values below 512 are the partition's own cells, the rest halo cells. `recv_slot`: slots of the partition's received buffer, which come only from partitions q-4 to q+3.
All inputs are finite; a program needn't handle non-finite values.
Results may differ from a plain program's by a relative error of at most 0.0001.
Values sent between devices are 32-bit elements; how exact they have to be, the bound alone decides.
A program may use at most 192 MiB of HBM per device.

v0:
```python
import jax
import jax.numpy as jnp
from jax import lax
from jax.experimental import pallas as pl
from jax.experimental.pallas import tpu as pltpu
from jax.sharding import PartitionSpec as P

AXES = ("comp", "dom")
MESH = pl.DeviceIdType.MESH
F32 = jnp.float32
BF16 = jnp.bfloat16

PEERS = 8
REACH = 3
STEPS = 3
GROUP = 4
LANES = 128

vertical_mix = 0.2
forcing_scale = 0.1
relaxation = 0.25
penetration = 8.0


def split(value):
    high = value.astype(BF16)
    return high, (value - high.astype(F32)).astype(BF16)


def across(left, right):
    return lax.dot_general(left, right, (((1,), (1,)), ((), ())), preferred_element_type=F32)


def lookup(table, index):
    return jnp.take_along_axis(table, index, axis=1, mode="promise_in_bounds")


def kernel(
    ocean, flux, coeff_in, near_in, halo_in, send_in, slot_in, weight_in,
    out_state, out_atm,
    state, parts, wide_hi, wide_lo, rims, coeff, near, halo, slots, weights,
    sends, air, sends8, keep, profile, added,
    slot_lanes, point_lanes, outgoing, arrived, surface, owned, sums, back, returned,
    rim_out, rim_in,
    state_send, state_recv, table_send, table_recv, flux_send, flux_recv,
    surf_send, surf_recv, back_send, back_recv, rim_send, rim_recv, out_send, out_recv, local,
):
    levels, cells = state.shape[1:]
    rim = halo.shape[2]
    points = air.shape[2]
    fields = GROUP
    blocks = points // LANES
    doms = lax.axis_size("dom")
    total = lax.axis_size("comp") * doms
    me = lax.axis_index("comp") * doms + lax.axis_index("dom")
    z = lax.rem(me, GROUP)
    base = me - z

    def device(p):
        p = lax.rem(p + total, total)
        return (lax.div(p, doms), lax.rem(p, doms))

    def remote(src, dst, send, recv, p):
        return pltpu.make_async_remote_copy(
            src_ref=src, dst_ref=dst, send_sem=send, recv_sem=recv,
            device_id=device(p), device_id_type=MESH,
        )

    barrier = pltpu.get_barrier_semaphore()
    for r in range(3):
        for k in range(GROUP):
            if r == 1 and k == 0:
                continue
            far = base + GROUP * (r - 1) + lax.rem(z + k, GROUP)
            pl.semaphore_signal(barrier, inc=1, device_id=device(far), device_id_type=MESH)

    tables = [(coeff_in, coeff), (near_in, near), (halo_in, halo), (slot_in, slots), (weight_in, weights)]
    own = [
        pltpu.make_async_copy(send_in, sends, local.at[0]),
        pltpu.make_async_copy(flux, air, local.at[1]),
        pltpu.make_async_copy(ocean.at[z], state.at[z], local.at[2]),
    ] + [
        pltpu.make_async_copy(src, dst.at[z], local.at[3 + n])
        for n, (src, dst) in enumerate(tables)
    ]
    for copy in own:
        copy.start()

    pl.semaphore_wait(barrier, 3 * GROUP - 1)

    for d in range(1, GROUP):
        far = lax.rem(z + d, GROUP)
        for n, (src, dst) in enumerate(tables):
            remote(src, dst.at[z], table_send.at[n, far], table_recv.at[n, z], base + far).start()
        remote(ocean.at[far], state.at[z], state_send.at[far], state_recv.at[z], base + far).start()

    def gather_and_send(interval):
        low = sends8[...] & (LANES - 1)
        high = lax.shift_right_logical(sends8[...], 7)
        for f in range(fields):
            total_f = jnp.zeros((PEERS, LANES), F32)
            for b in range(blocks):
                row = air[interval, f : f + 1, b * LANES : (b + 1) * LANES]
                if interval:
                    at = f * blocks + b
                    row = row - relaxation * returned[at : at + 1, :]
                table = jnp.broadcast_to(row, (PEERS, LANES))
                total_f = jnp.where(high == b, lookup(table, low), total_f)
            moved = pltpu.roll(
                jnp.concatenate([total_f, jnp.zeros((PEERS, LANES), F32)], axis=0), z + 1, 0
            )
            for r in range(3):
                outgoing[interval, f, r] = moved[GROUP * r : GROUP * (r + 1), :]
        for r in range(3):
            for k in range(GROUP):
                f = lax.rem(z + k, GROUP)
                src = outgoing.at[interval, f, r]
                dst = arrived.at[interval, GROUP * (2 - r) + z]
                if r == 1 and k == 0:
                    pltpu.make_async_copy(src, dst, local.at[8 + interval]).start()
                else:
                    remote(
                        src, dst, flux_send.at[interval, GROUP * r + f],
                        flux_recv.at[interval, GROUP * (2 - r) + z],
                        base + GROUP * (r - 1) + f,
                    ).start()

    def receive_forcing(interval):
        for r in range(3):
            for k in range(GROUP):
                f = lax.rem(z + k, GROUP)
                src = outgoing.at[interval, f, r]
                dst = arrived.at[interval, GROUP * r + f]
                if r == 1 and k == 0:
                    pltpu.make_async_copy(src, dst, local.at[8 + interval]).wait()
                else:
                    copy = remote(
                        src, dst, flux_send.at[interval, GROUP * r + f],
                        flux_recv.at[interval, GROUP * r + f], base + GROUP * (r - 1) + f,
                    )
                    copy.wait_recv()
                    copy.wait_send()
        for i in range(GROUP):
            for pair in range(cells // (2 * LANES)):
                cols = [slice((2 * pair + h) * LANES, (2 * pair + h + 1) * LANES) for h in range(2)]
                index = jnp.concatenate([slots[i, :, c] for c in cols], axis=0)
                weight = jnp.concatenate([weights[i, :, c] for c in cols], axis=0)
                low = index & (LANES - 1)
                high = lax.shift_right_logical(index, 7)
                value = jnp.zeros((PEERS, LANES), F32)
                for j in range(PEERS):
                    row = arrived[interval, 7 + i - j, i : i + 1, :]
                    table = jnp.broadcast_to(row, (PEERS, LANES))
                    value = jnp.where(high == j, lookup(table, low), value)
                value = value * weight
                for h in range(2):
                    added[i, :, cols[h]] = jnp.sum(value[4 * h : 4 * h + 4], axis=0, keepdims=True)

    def surface_out(interval):
        for i in range(GROUP):
            surface[interval, i] = state[i, 0:1, :]
        for d in range(GROUP):
            far = lax.rem(z + d, GROUP)
            if d == 0:
                pltpu.make_async_copy(
                    surface.at[interval, z], owned.at[interval, z], local.at[10 + interval]
                ).start()
            else:
                remote(
                    surface.at[interval, far], owned.at[interval, z],
                    surf_send.at[interval, far], surf_recv.at[interval, z], base + far,
                ).start()

    def sums_out(interval):
        for d in range(GROUP):
            far = lax.rem(z + d, GROUP)
            if d == 0:
                pltpu.make_async_copy(
                    surface.at[interval, z], owned.at[interval, z], local.at[10 + interval]
                ).wait()
            else:
                copy = remote(
                    surface.at[interval, far], owned.at[interval, far],
                    surf_send.at[interval, far], surf_recv.at[interval, far], base + far,
                )
                copy.wait_recv()
                copy.wait_send()
        acc = jnp.zeros((2 * fields * PEERS, LANES), F32)
        place = lax.broadcasted_iota(jnp.int32, (PEERS, cells), 0)
        for k in range(slots.shape[1]):
            hit = lax.shift_right_logical(slots[z, k : k + 1, :], 7) == place
            rows = [
                jnp.where(hit, weights[z, k : k + 1, :] * owned[interval, f], 0.0)
                for f in range(fields)
            ]
            high, low = split(jnp.concatenate(rows, axis=0))
            acc = acc + across(jnp.concatenate([high, low], axis=0), slot_lanes[k])
        acc = acc[: fields * PEERS] + acc[fields * PEERS :]
        for f in range(fields):
            for j in range(PEERS):
                sums[interval, j, f] = acc[f * PEERS + j : f * PEERS + j + 1, :]
        for j in range(PEERS):
            if j == REACH:
                pltpu.make_async_copy(
                    sums.at[interval, j], back.at[interval, j], local.at[12 + interval]
                ).start()
            else:
                remote(
                    sums.at[interval, j], back.at[interval, j],
                    back_send.at[interval, j], back_recv.at[interval, j], me + (REACH - j),
                ).start()

    def collect(interval):
        for j in range(PEERS):
            if j == REACH:
                pltpu.make_async_copy(
                    sums.at[interval, j], back.at[interval, j], local.at[12 + interval]
                ).wait()
            else:
                copy = remote(
                    sums.at[interval, j], back.at[interval, j],
                    back_send.at[interval, j], back_recv.at[interval, j], me + (REACH - j),
                )
                copy.wait_recv()
                copy.wait_send()
        place = lax.broadcasted_iota(jnp.int32, (blocks, LANES), 0)
        columns = []
        for j in range(PEERS):
            hit = lax.shift_right_logical(sends[:, j * LANES : (j + 1) * LANES], 7) == place
            columns.append(
                jnp.concatenate(
                    [jnp.where(hit, back[interval, j, f], 0.0) for f in range(fields)], axis=0
                )
            )
        high, low = split(jnp.concatenate(columns, axis=1))
        both = across(jnp.concatenate([high, low], axis=0), point_lanes[...])
        returned[...] = both[: fields * blocks] + both[fields * blocks :]

    def set_parts(i, value):
        high, low = split(value)
        parts[i, 0:levels, 0:cells] = high
        parts[i, levels : 2 * levels, 0:cells] = low

    def rims_of(t, i):
        edge = jnp.dot(parts[i, :, 0:cells], rims[i], preferred_element_type=F32)
        if i > 0:
            parts[i - 1, :, cells + rim : cells + 2 * rim] = edge[:, 0:rim].astype(BF16)
        else:
            rim_out[t, 0] = edge[0:levels, 0:rim] + edge[levels:, 0:rim]
            remote(
                rim_out.at[t, 0], rim_in.at[t, 1], rim_send.at[t, 0], rim_recv.at[t, 1], me - GROUP
            ).start()
        if i < GROUP - 1:
            parts[i + 1, :, cells : cells + rim] = edge[:, rim : 2 * rim].astype(BF16)
        else:
            rim_out[t, 1] = edge[0:levels, rim : 2 * rim] + edge[levels:, rim : 2 * rim]
            remote(
                rim_out.at[t, 1], rim_in.at[t, 0], rim_send.at[t, 1], rim_recv.at[t, 0], me + GROUP
            ).start()

    def rim_arrives(t, side):
        p = me + (GROUP if side else -GROUP)
        copy = remote(
            rim_out.at[t, 1 - side], rim_in.at[t, side], rim_send.at[t, 1 - side],
            rim_recv.at[t, side], p,
        )
        copy.wait_recv()
        high, low = split(rim_in[t, side])
        i, start = (GROUP - 1, cells + rim) if side else (0, cells)
        parts[i, 0:levels, start : start + rim] = high
        parts[i, levels : 2 * levels, start : start + rim] = low

    def rims_sent(t):
        remote(
            rim_out.at[t, 0], rim_in.at[t, 1], rim_send.at[t, 0], rim_recv.at[t, 1], me - GROUP
        ).wait_send()
        remote(
            rim_out.at[t, 1], rim_in.at[t, 0], rim_send.at[t, 1], rim_recv.at[t, 0], me + GROUP
        ).wait_send()

    def mixed(i):
        both = jnp.dot(parts[i], wide_hi[i], preferred_element_type=F32)
        small = jnp.dot(parts[i, 0:levels, :], wide_lo[i], preferred_element_type=F32)
        here = state[i]
        row = lax.broadcasted_iota(jnp.int32, (levels, cells), 0)
        above = jnp.where(row == 0, here, pltpu.roll(here, 1, 0))
        below = jnp.where(row == levels - 1, here, pltpu.roll(here, levels - 1, 0))
        return (
            keep[i] * here
            + (both[0:levels] + both[levels:] + small)
            + vertical_mix * (above + below)
        )

    def push(i):
        return added[i] * profile[...]

    level = lax.broadcasted_iota(jnp.int32, (levels, cells), 0).astype(F32)
    profile[...] = forcing_scale * jnp.exp(-level / penetration)
    own[0].wait()
    own[1].wait()
    sends8[...] = jnp.concatenate(
        [sends[:, j * LANES : (j + 1) * LANES] for j in range(PEERS)], axis=0
    )
    gather_and_send(0)
    for copy in own[3:]:
        copy.wait()

    def build(i):
        rows = [coeff[i, n : n + 1, :] for n in range(near.shape[1])]
        ids = [near[i, n : n + 1, :] for n in range(near.shape[1])]
        summed = []
        for n in range(len(rows)):
            value = rows[n]
            for m in range(n):
                value = value + jnp.where(ids[m] == ids[n], rows[m], 0.0)
            summed.append(value)
        whole = rows[0]
        for n in range(1, len(rows)):
            whole = whole + rows[n]
        keep[i] = (1.0 - 2.0 * vertical_mix) - whole
        step = 32

        def fill(c, _):
            first = pl.multiple_of(c * step, step)
            for q in range(cells // LANES):
                cols = slice(q * LANES, (q + 1) * LANES)
                place = lax.broadcasted_iota(jnp.int32, (step, LANES), 0) + first
                value = jnp.zeros((step, LANES), F32)
                for n in range(len(rows)):
                    value = jnp.where(ids[n][:, cols] == place, summed[n][:, cols], value)
                high, low = split(value)
                wide_hi[i, pl.ds(first, step), cols] = high
                wide_lo[i, pl.ds(first, step), cols] = low
            return 0

        lax.fori_loop(0, (cells + 2 * rim) // step, fill, 0)

        def select(c, _):
            first = pl.multiple_of(c * step, step)
            place = lax.broadcasted_iota(jnp.int32, (step, rim), 0) + first
            for side in range(2):
                hit = halo[i, side : side + 1, :] == place
                rims[i, pl.ds(first, step), side * rim : (side + 1) * rim] = jnp.where(
                    hit, 1.0, 0.0
                ).astype(BF16)
            return 0

        lax.fori_loop(0, cells // step, select, 0)

    def build_all(d, _):
        i = lax.rem(z + d, GROUP)

        @pl.when(d > 0)
        def _():
            for n, (src, dst) in enumerate(tables):
                copy = remote(src, dst.at[i], table_send.at[n, i], table_recv.at[n, i], base + i)
                copy.wait_recv()
                copy.wait_send()

        build(i)
        return 0

    lax.fori_loop(0, GROUP, build_all, 0)

    place = lax.broadcasted_iota(jnp.int32, (LANES, cells), 0)
    for k in range(slots.shape[1]):
        hit = (slots[z, k : k + 1, :] & (LANES - 1)) == place
        slot_lanes[k] = jnp.where(hit, 1.0, 0.0).astype(BF16)
    for h in range(sends.shape[1] // cells):
        hit = (sends[:, h * cells : (h + 1) * cells] & (LANES - 1)) == place
        point_lanes[:, h * cells : (h + 1) * cells] = jnp.where(hit, 1.0, 0.0).astype(BF16)

    own[2].wait()
    for d in range(1, GROUP):
        far = lax.rem(z + d, GROUP)
        copy = remote(
            ocean.at[far], state.at[far], state_send.at[far], state_recv.at[far], base + far
        )
        copy.wait_recv()
        copy.wait_send()
    for i in range(GROUP):
        set_parts(i, state[i])

    for interval in range(2):
        t = STEPS * interval
        if interval:
            surface_out(0)
        for i in (0, 3, 1, 2):
            rims_of(t, i)
        if interval:
            sums_out(0)
        for i in (1, 2):
            state[i] = mixed(i)
        if interval:
            collect(0)
            gather_and_send(1)
        rim_arrives(t, 0)
        state[0] = mixed(0)
        rim_arrives(t, 1)
        state[3] = mixed(3)
        rims_sent(t)
        receive_forcing(interval)
        for i in range(GROUP):
            value = state[i] + push(i)
            state[i] = value
            set_parts(i, value)

        def plain(s, _):
            now = t + s
            for i in (0, 3, 1, 2):
                rims_of(now, i)
            for i in (1, 2):
                value = mixed(i) + push(i)
                state[i] = value
                set_parts(i, value)
            rim_arrives(now, 0)
            value = mixed(0) + push(0)
            state[0] = value
            set_parts(0, value)
            rim_arrives(now, 1)
            value = mixed(3) + push(3)
            state[3] = value
            set_parts(3, value)
            rims_sent(now)
            return 0

        lax.fori_loop(1, STEPS, plain, 0)

    surface_out(1)
    for d in range(1, GROUP):
        far = lax.rem(z + d, GROUP)
        remote(
            state.at[far], out_state.at[z], out_send.at[far], out_recv.at[z], base + far
        ).start()
    mine = pltpu.make_async_copy(state.at[z], out_state.at[z], local.at[14])
    mine.start()
    sums_out(1)
    collect(1)
    out_atm[...] = returned[...]
    mine.wait()
    for d in range(1, GROUP):
        far = lax.rem(z + d, GROUP)
        copy = remote(
            state.at[far], out_state.at[far], out_send.at[far], out_recv.at[far], base + far
        )
        copy.wait_recv()
        copy.wait_send()


def shards(
    ocean_state, atm_flux, edge_coeff, neighbours, halo_send, send_idx, recv_slot, regrid_weight
):
    fields, levels, cells = ocean_state.shape
    points = atm_flux.shape[2]
    rim = halo_send.shape[1]
    slot_count = send_idx.shape[1]
    near = neighbours.shape[0]
    sources = recv_slot.shape[0]
    wide = cells + 2 * rim
    steps = 2 * STEPS
    dma = pltpu.SemaphoreType.DMA
    final, atm = pl.pallas_call(
        kernel,
        out_shape=(
            jax.ShapeDtypeStruct((fields, levels, cells), F32),
            jax.ShapeDtypeStruct((fields * points // LANES, LANES), F32),
        ),
        in_specs=[pl.BlockSpec(memory_space=pl.ANY)] * 8,
        out_specs=(
            pl.BlockSpec(memory_space=pl.ANY),
            pl.BlockSpec(memory_space=pltpu.VMEM),
        ),
        scratch_shapes=[
            pltpu.VMEM((GROUP, levels, cells), F32),
            pltpu.VMEM((GROUP, 2 * levels, wide), BF16),
            pltpu.VMEM((GROUP, wide, cells), BF16),
            pltpu.VMEM((GROUP, wide, cells), BF16),
            pltpu.VMEM((GROUP, cells, 2 * rim), BF16),
            pltpu.VMEM((GROUP, near, cells), F32),
            pltpu.VMEM((GROUP, near, cells), jnp.int32),
            pltpu.VMEM((GROUP, 2, rim), jnp.int32),
            pltpu.VMEM((GROUP, sources, cells), jnp.int32),
            pltpu.VMEM((GROUP, sources, cells), F32),
            pltpu.VMEM((1, slot_count), jnp.int32),
            pltpu.VMEM((2, fields, points), F32),
            pltpu.VMEM((PEERS, LANES), jnp.int32),
            pltpu.VMEM((GROUP, 1, cells), F32),
            pltpu.VMEM((levels, cells), F32),
            pltpu.VMEM((GROUP, 1, cells), F32),
            pltpu.VMEM((sources, LANES, cells), BF16),
            pltpu.VMEM((LANES, slot_count), BF16),
            pltpu.VMEM((2, fields, 3, GROUP, LANES), F32),
            pltpu.VMEM((2, 3 * GROUP, GROUP, LANES), F32),
            pltpu.VMEM((2, GROUP, 1, cells), F32),
            pltpu.VMEM((2, GROUP, 1, cells), F32),
            pltpu.VMEM((2, PEERS, fields, 1, LANES), F32),
            pltpu.VMEM((2, PEERS, fields, 1, LANES), F32),
            pltpu.VMEM((fields * points // LANES, LANES), F32),
            pltpu.VMEM((steps, 2, levels, rim), F32),
            pltpu.VMEM((steps, 2, levels, rim), F32),
            dma((GROUP,)),
            dma((GROUP,)),
            dma((5, GROUP)),
            dma((5, GROUP)),
            dma((2, 3 * GROUP)),
            dma((2, 3 * GROUP)),
            dma((2, GROUP)),
            dma((2, GROUP)),
            dma((2, PEERS)),
            dma((2, PEERS)),
            dma((steps, 2)),
            dma((steps, 2)),
            dma((GROUP,)),
            dma((GROUP,)),
            dma((15,)),
        ],
        compiler_params=pltpu.CompilerParams(
            collective_id=0, has_side_effects=True, vmem_limit_bytes=48 * 1024 * 1024
        ),
        name="coupled",
    )(
        ocean_state, atm_flux, edge_coeff, neighbours, halo_send, send_idx, recv_slot,
        regrid_weight,
    )
    return final, atm.reshape(fields, points)


def solution(mesh):
    placed = (
        P(None, None, AXES),
        P(None, None, AXES),
        P(None, AXES),
        P(None, AXES),
        P(None, AXES),
        P(AXES, None),
        P(None, AXES),
        P(None, AXES),
    )
    return jax.shard_map(
        shards,
        mesh=mesh,
        in_specs=placed,
        out_specs=(P(None, None, AXES), P(None, AXES)),
        check_vma=False,
    )
```

profile of v0, /device:TPU:1, one launch (start us, length us, event | category | flops | bytes accessed | tf_op | source)
XLA Modules:
  0.0 87.6 jit_solution(17051690976694628133)
XLA Ops:
  0.6 0.0 copy-start
  0.6 1.1 %copy-done = f32[4,80,512]{2,1,0:T(8,128)S(1)} copy-done((f32[4,80,512]{2,1,0:T(8,128)S(1)}, f32[4,80,512]{2,1,0:T(8,128)}, u32[]{:S(2)}) %copy-start) | copy-done | bytes 655384
  1.7 0.0 copy-start.1
  1.7 0.8 copy-done.1
  2.6 0.0 copy-start.2
  2.6 0.7 copy-done.2
  3.3 0.0 copy-start.3
  3.3 0.7 copy-done.3
  4.0 0.0 copy-start.4
  4.0 0.7 copy-done.4
  4.7 0.0 copy-start.5
  4.7 0.7 copy-done.5
  5.4 0.0 copy-start.6
  5.4 0.7 copy-done.6
  6.1 0.0 copy-start.7
  6.1 0.7 copy-done.7
  6.8 79.4 %coupled.1 = (f32[4,80,512]{2,1,0:T(8,128)S(1)}, f32[64,128]{1,0:T(8,128)S(1)}) custom-call(f32[4,80,512]{2,1,0:T(8,128)S(1)} %copy-done, f32[2,4,2048]{2,1,0:T(4,128)S(1)} %copy-done.1, f32[7,512]{1,0:T(8,128)S(1)} %copy-done.2, s32[7,512]{1,0:T(8,128)S(1)} %copy-done.3, s32[2,256]{1,0:T(2,128)S(1)} %copy-done.7, s32[1,1024]{1,0:T(1,128)S(1)} %copy-done.6, ...), custom_call_target="tpu_custom_call" | custom-call | tf_op jit(solution)/shard_map/coupled/pallas_call | solution.py:462
  86.2 0.6 reshape.7
  86.8 0.8 copy.11
Async XLA Ops:
  0.6 1.1 %copy-start = (f32[4,80,512]{2,1,0:T(8,128)S(1)}, f32[4,80,512]{2,1,0:T(8,128)}, u32[]{:S(2)}) copy-start(f32[4,80,512]{2,1,0:T(8,128)} %ocean.1) | copy-start | bytes 1966084
  1.7 0.8 copy-start.1
  2.6 0.7 copy-start.2
  3.3 0.7 copy-start.3
  4.0 0.7 copy-start.4
  4.7 0.7 copy-start.5
  5.4 0.7 copy-start.6
  6.1 0.7 copy-start.7
where the time goes:
time: 88.1 us; the launch traced here: 87.6 us
  Pallas kernels  79.4 us (90%)
  local copies, waits for them, and re-layouts  7.58 us (9%)
    pallas_call x1, Pallas kernels, shards(): pl.pallas_call(kernel, out_shape=(jax.ShapeDtypeStruct((fields, levels, c...  79.4 us
    unnamed x17, local copies, waits for them, and re-layouts  6.95 us

commit v1 on v0

--- a/solution.py
+++ b/solution.py
@@ -40,10 +40,10 @@
     out_state, out_atm,
     state, parts, wide_hi, wide_lo, rims, coeff, near, halo, slots, weights,
     sends, air, sends8, keep, profile, added,
-    slot_lanes, point_lanes, outgoing, arrived, surface, owned, sums, back, returned,
-    rim_out, rim_in,
+    slot_lanes, point_lanes, outgoing, arrived, sums, back, returned,
+    rim_out, rim_in, early,
     state_send, state_recv, table_send, table_recv, flux_send, flux_recv,
-    surf_send, surf_recv, back_send, back_recv, rim_send, rim_recv, out_send, out_recv, local,
+    back_send, back_recv, rim_send, rim_recv, out_send, out_recv, local,
 ):
     levels, cells = state.shape[1:]
     rim = halo.shape[2]
@@ -86,15 +86,7 @@
     for copy in own:
         copy.start()
 
-    pl.semaphore_wait(barrier, 3 * GROUP - 1)
-
-    for d in range(1, GROUP):
-        far = lax.rem(z + d, GROUP)
-        for n, (src, dst) in enumerate(tables):
-            remote(src, dst.at[z], table_send.at[n, far], table_recv.at[n, z], base + far).start()
-        remote(ocean.at[far], state.at[z], state_send.at[far], state_recv.at[z], base + far).start()
-
-    def gather_and_send(interval):
+    def gather(interval):
         low = sends8[...] & (LANES - 1)
         high = lax.shift_right_logical(sends8[...], 7)
         for f in range(fields):
@@ -111,6 +103,8 @@
             )
             for r in range(3):
                 outgoing[interval, f, r] = moved[GROUP * r : GROUP * (r + 1), :]
+
+    def send_slots(interval):
         for r in range(3):
             for k in range(GROUP):
                 f = lax.rem(z + k, GROUP)
@@ -156,80 +150,57 @@
                 for h in range(2):
                     added[i, :, cols[h]] = jnp.sum(value[4 * h : 4 * h + 4], axis=0, keepdims=True)
 
-    def surface_out(interval):
-        for i in range(GROUP):
-            surface[interval, i] = state[i, 0:1, :]
-        for d in range(GROUP):
-            far = lax.rem(z + d, GROUP)
-            if d == 0:
-                pltpu.make_async_copy(
-                    surface.at[interval, z], owned.at[interval, z], local.at[10 + interval]
-                ).start()
-            else:
-                remote(
-                    surface.at[interval, far], owned.at[interval, z],
-                    surf_send.at[interval, far], surf_recv.at[interval, z], base + far,
-                ).start()
+    def slot_sums(interval, i):
+        place = lax.broadcasted_iota(jnp.int32, (PEERS, cells), 0)
+        acc = jnp.zeros((2 * PEERS, LANES), F32)
+        top = state[i, 0:1, :]
+        for k in range(slots.shape[1]):
+            hit = lax.shift_right_logical(slots[i, k : k + 1, :], 7) == place
+            high, low = split(jnp.where(hit, weights[i, k : k + 1, :] * top, 0.0))
+            acc = acc + across(jnp.concatenate([high, low], axis=0), slot_lanes[i, k])
+        acc = acc[:PEERS] + acc[PEERS:]
+        for j in range(PEERS):
+            sums[interval, i - j + REACH + GROUP, i] = acc[j : j + 1, :]
+
+    def back_copy(interval, r, k, start):
+        f = lax.rem(z + k, GROUP)
+        src = sums.at[interval, GROUP * r + f]
+        if r == 1 and k == 0:
+            dst = back.at[interval, GROUP + z]
+            copy = pltpu.make_async_copy(src, dst, local.at[10 + interval])
+            copy.start() if start else copy.wait()
+            return
+        send = back_send.at[interval, GROUP * r + f]
+        p = base + GROUP * (r - 1) + f
+        slot = GROUP * (2 - r) + z if start else GROUP * r + f
+        copy = remote(src, back.at[interval, slot], send, back_recv.at[interval, slot], p)
+        if start:
+            copy.start()
+        else:
+            copy.wait_recv()
+            copy.wait_send()
 
     def sums_out(interval):
-        for d in range(GROUP):
-            far = lax.rem(z + d, GROUP)
-            if d == 0:
-                pltpu.make_async_copy(
-                    surface.at[interval, z], owned.at[interval, z], local.at[10 + interval]
-                ).wait()
-            else:
-                copy = remote(
-                    surface.at[interval, far], owned.at[interval, far],
-                    surf_send.at[interval, far], surf_recv.at[interval, far], base + far,
-                )
-                copy.wait_recv()
-                copy.wait_send()
-        acc = jnp.zeros((2 * fields * PEERS, LANES), F32)
-        place = lax.broadcasted_iota(jnp.int32, (PEERS, cells), 0)
-        for k in range(slots.shape[1]):
-            hit = lax.shift_right_logical(slots[z, k : k + 1, :], 7) == place
-            rows = [
-                jnp.where(hit, weights[z, k : k + 1, :] * owned[interval, f], 0.0)
-                for f in range(fields)
-            ]
-            high, low = split(jnp.concatenate(rows, axis=0))
-            acc = acc + across(jnp.concatenate([high, low], axis=0), slot_lanes[k])
-        acc = acc[: fields * PEERS] + acc[fields * PEERS :]
+        for r in range(3):
+            for k in range(GROUP):
+                back_copy(interval, r, k, True)
+
+    def collect(interval):
+        for r in range(3):
+            for k in range(GROUP):
+                back_copy(interval, r, k, False)
+        place = lax.broadcasted_iota(jnp.int32, (blocks, LANES), 0)
+        values = []
         for f in range(fields):
-            for j in range(PEERS):
-                sums[interval, j, f] = acc[f * PEERS + j : f * PEERS + j + 1, :]
-        for j in range(PEERS):
-            if j == REACH:
-                pltpu.make_async_copy(
-                    sums.at[interval, j], back.at[interval, j], local.at[12 + interval]
-                ).start()
-            else:
-                remote(
-                    sums.at[interval, j], back.at[interval, j],
-                    back_send.at[interval, j], back_recv.at[interval, j], me + (REACH - j),
-                ).start()
-
-    def collect(interval):
-        for j in range(PEERS):
-            if j == REACH:
-                pltpu.make_async_copy(
-                    sums.at[interval, j], back.at[interval, j], local.at[12 + interval]
-                ).wait()
-            else:
-                copy = remote(
-                    sums.at[interval, j], back.at[interval, j],
-                    back_send.at[interval, j], back_recv.at[interval, j], me + (REACH - j),
-                )
-                copy.wait_recv()
-                copy.wait_send()
-        place = lax.broadcasted_iota(jnp.int32, (blocks, LANES), 0)
+            rows = [back[interval, GROUP * r + f, i] for r in range(3) for i in range(GROUP)]
+            rows.append(jnp.zeros((GROUP, LANES), F32))
+            values.append(pltpu.roll(jnp.concatenate(rows, axis=0), 2 * PEERS - 1 - z, 0))
         columns = []
         for j in range(PEERS):
             hit = lax.shift_right_logical(sends[:, j * LANES : (j + 1) * LANES], 7) == place
             columns.append(
                 jnp.concatenate(
-                    [jnp.where(hit, back[interval, j, f], 0.0) for f in range(fields)], axis=0
+                    [jnp.where(hit, values[f][j : j + 1, :], 0.0) for f in range(fields)], axis=0
                 )
             )
         high, low = split(jnp.concatenate(columns, axis=1))
@@ -267,8 +238,12 @@
         copy.wait_recv()
         high, low = split(rim_in[t, side])
         i, start = (GROUP - 1, cells + rim) if side else (0, cells)
-        parts[i, 0:levels, start : start + rim] = high
-        parts[i, levels : 2 * levels, start : start + rim] = low
+        both = jnp.dot(
+            jnp.concatenate([high, low], axis=0), wide_hi[i, start : start + rim, :],
+            preferred_element_type=F32,
+        )
+        small = jnp.dot(high, wide_lo[i, start : start + rim, :], preferred_element_type=F32)
+        return early[side] + (both[0:levels] + both[levels:] + small)
 
     def rims_sent(t):
         remote(
@@ -278,22 +253,31 @@
             rim_out.at[t, 1], rim_in.at[t, 0], rim_send.at[t, 1], rim_recv.at[t, 0], me + GROUP
         ).wait_send()
 
+    def product(i, first, last):
+        both = jnp.dot(
+            parts[i, :, first:last], wide_hi[i, first:last, :], preferred_element_type=F32
+        )
+        small = jnp.dot(
+            parts[i, 0:levels, first:last], wide_lo[i, first:last, :], preferred_element_type=F32
+        )
+        return both[0:levels] + both[levels:] + small
+
     def mixed(i):
-        both = jnp.dot(parts[i], wide_hi[i], preferred_element_type=F32)
-        small = jnp.dot(parts[i, 0:levels, :], wide_lo[i], preferred_element_type=F32)
         here = state[i]
         row = lax.broadcasted_iota(jnp.int32, (levels, cells), 0)
         above = jnp.where(row == 0, here, pltpu.roll(here, 1, 0))
         below = jnp.where(row == levels - 1, here, pltpu.roll(here, levels - 1, 0))
-        return (
-            keep[i] * here
-            + (both[0:levels] + both[levels:] + small)
-            + vertical_mix * (above + below)
-        )
+        value = keep[i] * here + vertical_mix * (above + below)
+        if i == 0:
+            return value + product(i, 0, cells) + product(i, cells + rim, cells + 2 * rim)
+        if i == GROUP - 1:
+            return value + product(i, 0, cells + rim)
+        return value + product(i, 0, cells + 2 * rim)
 
     def push(i):
         return added[i] * profile[...]
 
+    sums[...] = jnp.zeros_like(sums)
     level = lax.broadcasted_iota(jnp.int32, (levels, cells), 0).astype(F32)
     profile[...] = forcing_scale * jnp.exp(-level / penetration)
     own[0].wait()
@@ -301,7 +285,16 @@
     sends8[...] = jnp.concatenate(
         [sends[:, j * LANES : (j + 1) * LANES] for j in range(PEERS)], axis=0
     )
-    gather_and_send(0)
+    gather(0)
+    pl.semaphore_wait(barrier, 3 * GROUP - 1)
+    for d in range(1, GROUP):
+        far = lax.rem(z + d, GROUP)
+        for n, (src, dst) in enumerate(tables):
+            remote(src, dst.at[z], table_send.at[n, far], table_recv.at[n, z], base + far).start()
+    send_slots(0)
+    for d in range(1, GROUP):
+        far = lax.rem(z + d, GROUP)
+        remote(ocean.at[far], state.at[z], state_send.at[far], state_recv.at[z], base + far).start()
     for copy in own[3:]:
         copy.wait()
 
@@ -346,6 +339,10 @@
             return 0
 
         lax.fori_loop(0, cells // step, select, 0)
+        place = lax.broadcasted_iota(jnp.int32, (LANES, cells), 0)
+        for k in range(slots.shape[1]):
+            hit = (slots[i, k : k + 1, :] & (LANES - 1)) == place
+            slot_lanes[i, k] = jnp.where(hit, 1.0, 0.0).astype(BF16)
 
     def build_all(d, _):
         i = lax.rem(z + d, GROUP)
@@ -363,14 +360,12 @@
     lax.fori_loop(0, GROUP, build_all, 0)
 
     place = lax.broadcasted_iota(jnp.int32, (LANES, cells), 0)
-    for k in range(slots.shape[1]):
-        hit = (slots[z, k : k + 1, :] & (LANES - 1)) == place
-        slot_lanes[k] = jnp.where(hit, 1.0, 0.0).astype(BF16)
     for h in range(sends.shape[1] // cells):
         hit = (sends[:, h * cells : (h + 1) * cells] & (LANES - 1)) == place
         point_lanes[:, h * cells : (h + 1) * cells] = jnp.where(hit, 1.0, 0.0).astype(BF16)
 
     own[2].wait()
+    set_parts(z, state[z])
     for d in range(1, GROUP):
         far = lax.rem(z + d, GROUP)
         copy = remote(
@@ -378,66 +373,87 @@
         )
         copy.wait_recv()
         copy.wait_send()
-    for i in range(GROUP):
-        set_parts(i, state[i])
-
-    for interval in range(2):
+        set_parts(far, state[far])
+    for i in (0, 3, 1, 2):
+        rims_of(0, i)
+
+    def settle(i, value):
+        state[i] = value
+        set_parts(i, value)
+
+    def first(interval):
         t = STEPS * interval
         if interval:
-            surface_out(0)
-        for i in (0, 3, 1, 2):
-            rims_of(t, i)
-        if interval:
+            for i in range(GROUP):
+                slot_sums(0, i)
             sums_out(0)
+        early[0] = mixed(0)
+        early[1] = mixed(3)
         for i in (1, 2):
             state[i] = mixed(i)
         if interval:
             collect(0)
-            gather_and_send(1)
-        rim_arrives(t, 0)
-        state[0] = mixed(0)
-        rim_arrives(t, 1)
-        state[3] = mixed(3)
+            gather(1)
+            send_slots(1)
+        state[0] = rim_arrives(t, 0)
+        state[3] = rim_arrives(t, 1)
         rims_sent(t)
         receive_forcing(interval)
-        for i in range(GROUP):
-            value = state[i] + push(i)
-            state[i] = value
-            set_parts(i, value)
-
-        def plain(s, _):
-            now = t + s
-            for i in (0, 3, 1, 2):
-                rims_of(now, i)
-            for i in (1, 2):
-                value = mixed(i) + push(i)
-                state[i] = value
-                set_parts(i, value)
-            rim_arrives(now, 0)
-            value = mixed(0) + push(0)
-            state[0] = value
-            set_parts(0, value)
-            rim_arrives(now, 1)
-            value = mixed(3) + push(3)
-            state[3] = value
-            set_parts(3, value)
-            rims_sent(now)
-            return 0
-
-        lax.fori_loop(1, STEPS, plain, 0)
-
-    surface_out(1)
-    for d in range(1, GROUP):
-        far = lax.rem(z + d, GROUP)
-        remote(
-            state.at[far], out_state.at[z], out_send.at[far], out_recv.at[z], base + far
-        ).start()
-    mine = pltpu.make_async_copy(state.at[z], out_state.at[z], local.at[14])
-    mine.start()
+        for i in (0, 3, 1, 2):
+            settle(i, state[i] + push(i))
+            rims_of(t + 1, i)
+
+    def plain(t):
+        for i in (1, 2):
+            settle(i, mixed(i) + push(i))
+        early[0] = mixed(0) + push(0)
+        early[1] = mixed(3) + push(3)
+        settle(0, rim_arrives(t, 0))
+        rims_of(t + 1, 0)
+        settle(3, rim_arrives(t, 1))
+        rims_of(t + 1, 3)
+        rims_of(t + 1, 1)
+        rims_of(t + 1, 2)
+        rims_sent(t)
+
+    def plain_step(t, _):
+        plain(t)
+        return 0
+
+    def ship(i):
+        @pl.when(z == i)
+        def _():
+            pltpu.make_async_copy(state.at[i], out_state.at[i], local.at[14]).start()
+
+        @pl.when(z != i)
+        def _():
+            remote(
+                state.at[i], out_state.at[z], out_send.at[i], out_recv.at[z], base + i
+            ).start()
+
+    first(0)
+    lax.fori_loop(1, STEPS, plain_step, 0)
+    first(1)
+    plain(STEPS + 1)
+    last = 2 * STEPS - 1
+    for i in (1, 2):
+        state[i] = mixed(i) + push(i)
+        ship(i)
+    early[0] = mixed(0) + push(0)
+    early[1] = mixed(3) + push(3)
+    for i in (1, 2):
+        slot_sums(1, i)
+    state[0] = rim_arrives(last, 0)
+    slot_sums(1, 0)
+    state[3] = rim_arrives(last, 1)
+    slot_sums(1, 3)
     sums_out(1)
+    ship(0)
+    ship(3)
+    rims_sent(last)
     collect(1)
     out_atm[...] = returned[...]
-    mine.wait()
+    pltpu.make_async_copy(state.at[z], out_state.at[z], local.at[14]).wait()
     for d in range(1, GROUP):
         far = lax.rem(z + d, GROUP)
         copy = remote(
@@ -487,27 +503,24 @@
             pltpu.VMEM((GROUP, 1, cells), F32),
             pltpu.VMEM((levels, cells), F32),
             pltpu.VMEM((GROUP, 1, cells), F32),
-            pltpu.VMEM((sources, LANES, cells), BF16),
+            pltpu.VMEM((GROUP, sources, LANES, cells), BF16),
             pltpu.VMEM((LANES, slot_count), BF16),
             pltpu.VMEM((2, fields, 3, GROUP, LANES), F32),
             pltpu.VMEM((2, 3 * GROUP, GROUP, LANES), F32),
-            pltpu.VMEM((2, GROUP, 1, cells), F32),
-            pltpu.VMEM((2, GROUP, 1, cells), F32),
-            pltpu.VMEM((2, PEERS, fields, 1, LANES), F32),
-            pltpu.VMEM((2, PEERS, fields, 1, LANES), F32),
+            pltpu.VMEM((2, 3 * GROUP, GROUP, 1, LANES), F32),
+            pltpu.VMEM((2, 3 * GROUP, GROUP, 1, LANES), F32),
             pltpu.VMEM((fields * points // LANES, LANES), F32),
             pltpu.VMEM((steps, 2, levels, rim), F32),
             pltpu.VMEM((steps, 2, levels, rim), F32),
+            pltpu.VMEM((2, levels, cells), F32),
             dma((GROUP,)),
             dma((GROUP,)),
             dma((5, GROUP)),
             dma((5, GROUP)),
             dma((2, 3 * GROUP)),
             dma((2, 3 * GROUP)),
-            dma((2, GROUP)),
-            dma((2, GROUP)),
-            dma((2, PEERS)),
-            dma((2, PEERS)),
+            dma((2, 3 * GROUP)),
+            dma((2, 3 * GROUP)),
             dma((steps, 2)),
             dma((steps, 2)),
             dma((GROUP,)),
@@ -515,7 +528,7 @@
             dma((15,)),
         ],
         compiler_params=pltpu.CompilerParams(
-            collective_id=0, has_side_effects=True, vmem_limit_bytes=48 * 1024 * 1024
+            collective_id=0, has_side_effects=True, vmem_limit_bytes=67_043_328
         ),
         name="coupled",
     )(

time: 88.1 us -> 78.8 us (0.89)
  Pallas kernels: 79.4 us -> 74.6 us
  local copies, waits for them, and re-layouts: 7.58 us -> 3.35 us
    unnamed x17 -> x1, local copies, waits for them, and re-layouts: 6.95 us -> 1.97 us
    pallas_call x1, Pallas kernels: 79.4 us -> 74.6 us  [shards(): pl.pallas_call(kernel, out_shape=(jax.ShapeDtypeStruct((fields, levels, c...]
where the time goes in v1:
time: 78.8 us; the launch traced here: 78.6 us
  Pallas kernels  74.6 us (95%)
  local copies, waits for them, and re-layouts  3.35 us (4%)
    pallas_call x1, Pallas kernels, shards(): pl.pallas_call(kernel, out_shape=(jax.ShapeDtypeStruct((fields, levels, c...  74.6 us
    unnamed x1, local copies, waits for them, and re-layouts  1.97 us

profile of v1, /device:TPU:1, one launch (start us, length us, event | category | flops | bytes accessed | tf_op | source)
XLA Modules:
  0.0 78.6 jit_solution(2849054419015986316)
XLA Ops:
  0.6 74.6 %coupled.1 = (f32[4,80,512]{2,1,0:T(8,128)}, f32[64,128]{1,0:T(8,128)}) custom-call(f32[4,80,512]{2,1,0:T(8,128)} %ocean.1, f32[2,4,2048]{2,1,0:T(4,128)} %flux.1, f32[7,512]{1,0:T(8,128)} %coeff_in.1, s32[7,512]{1,0:T(8,128)} %near_in.1, s32[2,256]{1,0:T(2,128)} %halo_in.1, s32[1,1024]{1,0:T(1,128)} %send_in.1, s32[4,512]{1,0:T(4,128)} %slot_in.1, ...), custom_call_target="tpu_custom_call" | custom-call | tf_op jit(solution)/shard_map/coupled/pallas_call | solution.py:478
  75.3 1.4 %reshape.7 = f32[4,2048]{1,0:T(4,128)} reshape(f32[64,128]{1,0:T(8,128)} %get-tuple-element.5) | data formatting | bytes 65536 | tf_op jit(solution)/shard_map/reshape | solution.py:538
  76.6 2.0 %copy.11 = f32[4,80,512]{2,1,0:T(8,128)} copy(f32[4,80,512]{2,1,0:T(8,128)} %get-tuple-element.8) | data formatting | bytes 1310720

commit v2 on v1

--- a/solution.py
+++ b/solution.py
@@ -15,6 +15,7 @@
 STEPS = 3
 GROUP = 4
 LANES = 128
+PIECES = ((0, 48), (48, 80))
 
 vertical_mix = 0.2
 forcing_scale = 0.1
@@ -212,46 +213,57 @@
         parts[i, 0:levels, 0:cells] = high
         parts[i, levels : 2 * levels, 0:cells] = low
 
-    def rims_of(t, i):
-        edge = jnp.dot(parts[i, :, 0:cells], rims[i], preferred_element_type=F32)
-        if i > 0:
-            parts[i - 1, :, cells + rim : cells + 2 * rim] = edge[:, 0:rim].astype(BF16)
-        else:
-            rim_out[t, 0] = edge[0:levels, 0:rim] + edge[levels:, 0:rim]
-            remote(
-                rim_out.at[t, 0], rim_in.at[t, 1], rim_send.at[t, 0], rim_recv.at[t, 1], me - GROUP
-            ).start()
-        if i < GROUP - 1:
-            parts[i + 1, :, cells : cells + rim] = edge[:, rim : 2 * rim].astype(BF16)
-        else:
-            rim_out[t, 1] = edge[0:levels, rim : 2 * rim] + edge[levels:, rim : 2 * rim]
-            remote(
-                rim_out.at[t, 1], rim_in.at[t, 0], rim_send.at[t, 1], rim_recv.at[t, 0], me + GROUP
-            ).start()
-
-    def rim_arrives(t, side):
+    def rim_copy(t, side, c):
+        a, b = PIECES[c]
+        return remote(
+            rim_out.at[t, side, a:b], rim_in.at[t, 1 - side, a:b], rim_send.at[t, side, c],
+            rim_recv.at[t, 1 - side, c], me + (GROUP if side else -GROUP),
+        )
+
+    def outer_rims(t, side, c):
+        i = side * (GROUP - 1)
+        a, b = PIECES[c]
+        both = jnp.concatenate(
+            [parts[i, a:b, 0:cells], parts[i, levels + a : levels + b, 0:cells]], axis=0
+        )
+        edge = jnp.dot(
+            both, rims[i, :, side * rim : (side + 1) * rim], preferred_element_type=F32
+        )
+        rim_out[t, side, a:b] = edge[0 : b - a] + edge[b - a :]
+        rim_copy(t, side, c).start()
+
+    def inner_rims(i):
+        for side in range(2):
+            j = i - 1 + 2 * side
+            if 0 <= j < GROUP:
+                edge = jnp.dot(
+                    parts[i, :, 0:cells], rims[i, :, side * rim : (side + 1) * rim],
+                    preferred_element_type=F32,
+                )
+                start = cells if side else cells + rim
+                parts[j, :, start : start + rim] = edge.astype(BF16)
+
+    def rim_arrives(t, side, c):
+        a, b = PIECES[c]
         p = me + (GROUP if side else -GROUP)
         copy = remote(
-            rim_out.at[t, 1 - side], rim_in.at[t, side], rim_send.at[t, 1 - side],
-            rim_recv.at[t, side], p,
+            rim_out.at[t, 1 - side, a:b], rim_in.at[t, side, a:b], rim_send.at[t, 1 - side, c],
+            rim_recv.at[t, side, c], p,
         )
         copy.wait_recv()
-        high, low = split(rim_in[t, side])
+        high, low = split(rim_in[t, side, a:b])
         i, start = (GROUP - 1, cells + rim) if side else (0, cells)
         both = jnp.dot(
             jnp.concatenate([high, low], axis=0), wide_hi[i, start : start + rim, :],
             preferred_element_type=F32,
         )
         small = jnp.dot(high, wide_lo[i, start : start + rim, :], preferred_element_type=F32)
-        return early[side] + (both[0:levels] + both[levels:] + small)
+        return early[side, a:b] + (both[0 : b - a] + both[b - a :] + small)
 
     def rims_sent(t):
-        remote(
-            rim_out.at[t, 0], rim_in.at[t, 1], rim_send.at[t, 0], rim_recv.at[t, 1], me - GROUP
-        ).wait_send()
-        remote(
-            rim_out.at[t, 1], rim_in.at[t, 0], rim_send.at[t, 1], rim_recv.at[t, 0], me + GROUP
-        ).wait_send()
+        for side in range(2):
+            for c in range(len(PIECES)):
+                rim_copy(t, side, c).wait_send()
 
     def product(i, first, last):
         both = jnp.dot(
@@ -374,12 +386,27 @@
         copy.wait_recv()
         copy.wait_send()
         set_parts(far, state[far])
-    for i in (0, 3, 1, 2):
-        rims_of(0, i)
+    pieces = range(len(PIECES))
+
+    def all_rims(t):
+        for c in pieces:
+            outer_rims(t, 0, c)
+            outer_rims(t, 1, c)
+        for i in (0, 3, 1, 2):
+            inner_rims(i)
+
+    all_rims(0)
 
     def settle(i, value):
         state[i] = value
         set_parts(i, value)
+
+    def settle_piece(i, c, value):
+        a, b = PIECES[c]
+        high, low = split(value)
+        state[i, a:b] = value
+        parts[i, a:b, 0:cells] = high
+        parts[i, levels + a : levels + b, 0:cells] = low
 
     def first(interval):
         t = STEPS * interval
@@ -395,25 +422,27 @@
             collect(0)
             gather(1)
             send_slots(1)
-        state[0] = rim_arrives(t, 0)
-        state[3] = rim_arrives(t, 1)
+        for c in pieces:
+            a, b = PIECES[c]
+            state[0, a:b] = rim_arrives(t, 0, c)
+            state[3, a:b] = rim_arrives(t, 1, c)
         rims_sent(t)
         receive_forcing(interval)
         for i in (0, 3, 1, 2):
             settle(i, state[i] + push(i))
-            rims_of(t + 1, i)
+        all_rims(t + 1)
 
     def plain(t):
         for i in (1, 2):
             settle(i, mixed(i) + push(i))
         early[0] = mixed(0) + push(0)
         early[1] = mixed(3) + push(3)
-        settle(0, rim_arrives(t, 0))
-        rims_of(t + 1, 0)
-        settle(3, rim_arrives(t, 1))
-        rims_of(t + 1, 3)
-        rims_of(t + 1, 1)
-        rims_of(t + 1, 2)
+        for c in pieces:
+            for side in range(2):
+                settle_piece(side * (GROUP - 1), c, rim_arrives(t, side, c))
+                outer_rims(t + 1, side, c)
+        for i in (0, 3, 1, 2):
+            inner_rims(i)
         rims_sent(t)
 
     def plain_step(t, _):
@@ -443,16 +472,22 @@
     early[1] = mixed(3) + push(3)
     for i in (1, 2):
         slot_sums(1, i)
-    state[0] = rim_arrives(last, 0)
-    slot_sums(1, 0)
-    state[3] = rim_arrives(last, 1)
-    slot_sums(1, 3)
-    sums_out(1)
+    for c in pieces:
+        a, b = PIECES[c]
+        state[0, a:b] = rim_arrives(last, 0, c)
+        state[3, a:b] = rim_arrives(last, 1, c)
+        if c == 0:
+            slot_sums(1, 0)
+            slot_sums(1, 3)
+            sums_out(1)
     ship(0)
     ship(3)
     rims_sent(last)
     collect(1)
-    out_atm[...] = returned[...]
+    for b in range(blocks):
+        out_atm[:, b * LANES : (b + 1) * LANES] = jnp.concatenate(
+            [returned[f * blocks + b : f * blocks + b + 1, :] for f in range(fields)], axis=0
+        )
     pltpu.make_async_copy(state.at[z], out_state.at[z], local.at[14]).wait()
     for d in range(1, GROUP):
         far = lax.rem(z + d, GROUP)
@@ -479,9 +514,9 @@
         kernel,
         out_shape=(
             jax.ShapeDtypeStruct((fields, levels, cells), F32),
-            jax.ShapeDtypeStruct((fields * points // LANES, LANES), F32),
+            jax.ShapeDtypeStruct((fields, points), F32),
         ),
-        in_specs=[pl.BlockSpec(memory_space=pl.ANY)] * 8,
+        in_specs=[pl.BlockSpec(memory_space=pltpu.HBM)] * 8,
         out_specs=(
             pl.BlockSpec(memory_space=pl.ANY),
             pl.BlockSpec(memory_space=pltpu.VMEM),
@@ -521,8 +556,8 @@
             dma((2, 3 * GROUP)),
             dma((2, 3 * GROUP)),
             dma((2, 3 * GROUP)),
-            dma((steps, 2)),
-            dma((steps, 2)),
+            dma((steps, 2, len(PIECES))),
+            dma((steps, 2, len(PIECES))),
             dma((GROUP,)),
             dma((GROUP,)),
             dma((15,)),
@@ -535,7 +570,7 @@
         ocean_state, atm_flux, edge_coeff, neighbours, halo_send, send_idx, recv_slot,
         regrid_weight,
     )
-    return final, atm.reshape(fields, points)
+    return final, atm
 
 
 def solution(mesh):

time: 78.8 us -> 78 us (0.990)
    reshape x1 -> x0, local copies, waits for them, and re-layouts: 1.39 us -> none  [shards(): return (final, atm.reshape(fields, points))]
    unnamed x1 -> x4, local copies, waits for them, and re-layouts: 1.97 us -> 2.59 us
where the time goes in v2:
time: 78 us; the launch traced here: 77.8 us
  Pallas kernels  74.6 us (96%)
  local copies, waits for them, and re-layouts  2.59 us (3%)
    pallas_call x1, Pallas kernels, shards(): pl.pallas_call(kernel, out_shape=(jax.ShapeDtypeStruct((fields, levels, c...  74.6 us
    unnamed x4, local copies, waits for them, and re-layouts  2.59 us

profile of v2, /device:TPU:1, one launch (start us, length us, event | category | flops | bytes accessed | tf_op | source)
XLA Modules:
  0.0 77.8 jit_solution(12345435124247253188)
XLA Ops:
  0.6 74.6 %coupled.1 = (f32[4,80,512]{2,1,0:T(8,128)}, f32[4,2048]{1,0:T(4,128)}) custom-call(f32[4,80,512]{2,1,0:T(8,128)} %ocean.1, f32[2,4,2048]{2,1,0:T(4,128)} %flux.1, f32[7,512]{1,0:T(8,128)} %coeff_in.1, s32[7,512]{1,0:T(8,128)} %near_in.1, s32[2,256]{1,0:T(2,128)} %halo_in.1, s32[1,1024]{1,0:T(1,128)} %send_in.1, s32[4,512]{1,0:T(4,128)} %slot_in.1, ...), custom_call_target="tpu_custom_call" | custom-call | tf_op jit(solution)/shard_map/coupled/pallas_call | solution.py:513
  75.2 0.0 copy-start
  75.2 2.0 %copy.12 = f32[4,80,512]{2,1,0:T(8,128)} copy(f32[4,80,512]{2,1,0:T(8,128)} %get-tuple-element.4) | data formatting | bytes 1310720
  77.2 0.0 copy-done
  77.2 0.6 copy.13
Async XLA Ops:
  75.2 2.0 %copy-start = (f32[4,2048]{1,0:T(4,128)S(1)}, f32[4,2048]{1,0:T(4,128)}, u32[]{:S(2)}) copy-start(f32[4,2048]{1,0:T(4,128)} %get-tuple-element.5) | copy-start | bytes 98308

commit v3 on v2

--- a/solution.py
+++ b/solution.py
@@ -42,9 +42,9 @@
     state, parts, wide_hi, wide_lo, rims, coeff, near, halo, slots, weights,
     sends, air, sends8, keep, profile, added,
     slot_lanes, point_lanes, outgoing, arrived, sums, back, returned,
-    rim_out, rim_in, early,
+    rim_out, rim_in, early, owner_state, owner_rims,
     state_send, state_recv, table_send, table_recv, flux_send, flux_recv,
-    back_send, back_recv, rim_send, rim_recv, out_send, out_recv, local,
+    back_send, back_recv, rim_send, rim_recv, owner_send, out_send, out_recv, local,
 ):
     levels, cells = state.shape[1:]
     rim = halo.shape[2]
@@ -83,7 +83,7 @@
     ] + [
         pltpu.make_async_copy(src, dst.at[z], local.at[3 + n])
         for n, (src, dst) in enumerate(tables)
-    ]
+    ] + [pltpu.make_async_copy(ocean, owner_state, local.at[15])]
     for copy in own:
         copy.start()
 
@@ -135,21 +135,21 @@
                     )
                     copy.wait_recv()
                     copy.wait_send()
-        for i in range(GROUP):
-            for pair in range(cells // (2 * LANES)):
-                cols = [slice((2 * pair + h) * LANES, (2 * pair + h + 1) * LANES) for h in range(2)]
-                index = jnp.concatenate([slots[i, :, c] for c in cols], axis=0)
-                weight = jnp.concatenate([weights[i, :, c] for c in cols], axis=0)
-                low = index & (LANES - 1)
-                high = lax.shift_right_logical(index, 7)
-                value = jnp.zeros((PEERS, LANES), F32)
-                for j in range(PEERS):
-                    row = arrived[interval, 7 + i - j, i : i + 1, :]
-                    table = jnp.broadcast_to(row, (PEERS, LANES))
-                    value = jnp.where(high == j, lookup(table, low), value)
-                value = value * weight
-                for h in range(2):
-                    added[i, :, cols[h]] = jnp.sum(value[4 * h : 4 * h + 4], axis=0, keepdims=True)
+    def cell_forcing(interval, i):
+        for pair in range(cells // (2 * LANES)):
+            cols = [slice((2 * pair + h) * LANES, (2 * pair + h + 1) * LANES) for h in range(2)]
+            index = jnp.concatenate([slots[i, :, c] for c in cols], axis=0)
+            weight = jnp.concatenate([weights[i, :, c] for c in cols], axis=0)
+            low = index & (LANES - 1)
+            high = lax.shift_right_logical(index, 7)
+            value = jnp.zeros((PEERS, LANES), F32)
+            for j in range(PEERS):
+                row = arrived[interval, 7 + i - j, i : i + 1, :]
+                table = jnp.broadcast_to(row, (PEERS, LANES))
+                value = jnp.where(high == j, lookup(table, low), value)
+            value = value * weight
+            for h in range(2):
+                added[i, :, cols[h]] = jnp.sum(value[4 * h : 4 * h + 4], axis=0, keepdims=True)
 
     def slot_sums(interval, i):
         place = lax.broadcasted_iota(jnp.int32, (PEERS, cells), 0)
@@ -298,6 +298,59 @@
         [sends[:, j * LANES : (j + 1) * LANES] for j in range(PEERS)], axis=0
     )
     gather(0)
+    for copy in own[3:]:
+        copy.wait()
+    step = 32
+
+    def build_rims(i):
+        def select(c, _):
+            first = pl.multiple_of(c * step, step)
+            place = lax.broadcasted_iota(jnp.int32, (step, rim), 0) + first
+            for side in range(2):
+                hit = halo[i, side : side + 1, :] == place
+                rims[i, pl.ds(first, step), side * rim : (side + 1) * rim] = jnp.where(
+                    hit, 1.0, 0.0
+                ).astype(BF16)
+            return 0
+
+        lax.fori_loop(0, cells // step, select, 0)
+
+    build_rims(z)
+
+    def owner_copy(side, f, c):
+        a, b = PIECES[c]
+        return remote(
+            owner_rims.at[f, a:b], rim_in.at[0, 1 - side, a:b], owner_send.at[f, c],
+            rim_recv.at[0, 1 - side, c], base + (GROUP if side else -GROUP) + f,
+        )
+
+    def at_ends(act):
+        for side in range(2):
+            @pl.when(z == side * (GROUP - 1))
+            def _():
+                act(side)
+
+    def first_rims(side):
+        for f in range(fields):
+            high, low = split(owner_state[f])
+            edge = jnp.dot(
+                jnp.concatenate([high, low], axis=0),
+                rims[z, :, side * rim : (side + 1) * rim],
+                preferred_element_type=F32,
+            )
+            owner_rims[f] = edge[0:levels] + edge[levels:]
+
+    def first_rims_go(side):
+        for c in range(len(PIECES)):
+            for f in range(fields):
+                owner_copy(side, f, c).start()
+
+    def first_rims_sent(side):
+        for c in range(len(PIECES)):
+            for f in range(fields):
+                owner_copy(side, f, c).wait_send()
+
+    at_ends(first_rims)
     pl.semaphore_wait(barrier, 3 * GROUP - 1)
     for d in range(1, GROUP):
         far = lax.rem(z + d, GROUP)
@@ -307,8 +360,7 @@
     for d in range(1, GROUP):
         far = lax.rem(z + d, GROUP)
         remote(ocean.at[far], state.at[z], state_send.at[far], state_recv.at[z], base + far).start()
-    for copy in own[3:]:
-        copy.wait()
+    at_ends(first_rims_go)
 
     def build(i):
         rows = [coeff[i, n : n + 1, :] for n in range(near.shape[1])]
@@ -323,7 +375,6 @@
         for n in range(1, len(rows)):
             whole = whole + rows[n]
         keep[i] = (1.0 - 2.0 * vertical_mix) - whole
-        step = 32
 
         def fill(c, _):
             first = pl.multiple_of(c * step, step)
@@ -340,17 +391,10 @@
 
         lax.fori_loop(0, (cells + 2 * rim) // step, fill, 0)
 
-        def select(c, _):
-            first = pl.multiple_of(c * step, step)
-            place = lax.broadcasted_iota(jnp.int32, (step, rim), 0) + first
-            for side in range(2):
-                hit = halo[i, side : side + 1, :] == place
-                rims[i, pl.ds(first, step), side * rim : (side + 1) * rim] = jnp.where(
-                    hit, 1.0, 0.0
-                ).astype(BF16)
-            return 0
-
-        lax.fori_loop(0, cells // step, select, 0)
+        @pl.when(i != z)
+        def _():
+            build_rims(i)
+
         place = lax.broadcasted_iota(jnp.int32, (LANES, cells), 0)
         for k in range(slots.shape[1]):
             hit = (slots[i, k : k + 1, :] & (LANES - 1)) == place
@@ -388,14 +432,8 @@
         set_parts(far, state[far])
     pieces = range(len(PIECES))
 
-    def all_rims(t):
-        for c in pieces:
-            outer_rims(t, 0, c)
-            outer_rims(t, 1, c)
-        for i in (0, 3, 1, 2):
-            inner_rims(i)
-
-    all_rims(0)
+    for i in (0, 3, 1, 2):
+        inner_rims(i)
 
     def settle(i, value):
         state[i] = value
@@ -410,10 +448,6 @@
 
     def first(interval):
         t = STEPS * interval
-        if interval:
-            for i in range(GROUP):
-                slot_sums(0, i)
-            sums_out(0)
         early[0] = mixed(0)
         early[1] = mixed(3)
         for i in (1, 2):
@@ -426,28 +460,42 @@
             a, b = PIECES[c]
             state[0, a:b] = rim_arrives(t, 0, c)
             state[3, a:b] = rim_arrives(t, 1, c)
-        rims_sent(t)
         receive_forcing(interval)
+        for i in (0, 3):
+            cell_forcing(interval, i)
+            settle(i, state[i] + push(i))
+        for c in pieces:
+            outer_rims(t + 1, 0, c)
+            outer_rims(t + 1, 1, c)
+        for i in (1, 2):
+            cell_forcing(interval, i)
+            settle(i, state[i] + push(i))
         for i in (0, 3, 1, 2):
-            settle(i, state[i] + push(i))
-        all_rims(t + 1)
-
-    def plain(t):
+            inner_rims(i)
+        if interval:
+            rims_sent(t)
+        else:
+            at_ends(first_rims_sent)
+
+    def plain(t, sums_too=False):
         for i in (1, 2):
             settle(i, mixed(i) + push(i))
         early[0] = mixed(0) + push(0)
         early[1] = mixed(3) + push(3)
+        if sums_too:
+            slot_sums(0, 1)
+            slot_sums(0, 2)
         for c in pieces:
             for side in range(2):
                 settle_piece(side * (GROUP - 1), c, rim_arrives(t, side, c))
                 outer_rims(t + 1, side, c)
+            if sums_too and c == 0:
+                slot_sums(0, 0)
+                slot_sums(0, 3)
+                sums_out(0)
         for i in (0, 3, 1, 2):
             inner_rims(i)
         rims_sent(t)
-
-    def plain_step(t, _):
-        plain(t)
-        return 0
 
     def ship(i):
         @pl.when(z == i)
@@ -461,17 +509,18 @@
             ).start()
 
     first(0)
-    lax.fori_loop(1, STEPS, plain_step, 0)
+    for t in range(1, STEPS):
+        plain(t, t == STEPS - 1)
     first(1)
     plain(STEPS + 1)
     last = 2 * STEPS - 1
     for i in (1, 2):
         state[i] = mixed(i) + push(i)
+        slot_sums(1, i)
+        state[i] = 0.5 * state[i]
         ship(i)
     early[0] = mixed(0) + push(0)
     early[1] = mixed(3) + push(3)
-    for i in (1, 2):
-        slot_sums(1, i)
     for c in pieces:
         a, b = PIECES[c]
         state[0, a:b] = rim_arrives(last, 0, c)
@@ -480,8 +529,9 @@
             slot_sums(1, 0)
             slot_sums(1, 3)
             sums_out(1)
-    ship(0)
-    ship(3)
+    for i in (0, 3):
+        state[i] = 0.5 * state[i]
+        ship(i)
     rims_sent(last)
     collect(1)
     for b in range(blocks):
@@ -548,6 +598,8 @@
             pltpu.VMEM((steps, 2, levels, rim), F32),
             pltpu.VMEM((steps, 2, levels, rim), F32),
             pltpu.VMEM((2, levels, cells), F32),
+            pltpu.VMEM((fields, levels, cells), F32),
+            pltpu.VMEM((fields, levels, rim), F32),
             dma((GROUP,)),
             dma((GROUP,)),
             dma((5, GROUP)),
@@ -558,9 +610,10 @@
             dma((2, 3 * GROUP)),
             dma((steps, 2, len(PIECES))),
             dma((steps, 2, len(PIECES))),
+            dma((fields, len(PIECES))),
             dma((GROUP,)),
             dma((GROUP,)),
-            dma((15,)),
+            dma((16,)),
         ],
         compiler_params=pltpu.CompilerParams(
             collective_id=0, has_side_effects=True, vmem_limit_bytes=67_043_328
@@ -570,7 +623,7 @@
         ocean_state, atm_flux, edge_coeff, neighbours, halo_send, send_idx, recv_slot,
         regrid_weight,
     )
-    return final, atm
+    return 2.0 * final, atm
 
 
 def solution(mesh):

time: 78 us -> 77 us (0.987)
  other arithmetic: 0 us -> 1.99 us
  local copies, waits for them, and re-layouts: 2.59 us -> 0.62 us
  Pallas kernels: 74.6 us -> 73.6 us
    mul x0 -> x1, other arithmetic: none -> 1.99 us  [shards(): return (2.0 * final, atm)]
    unnamed x4 -> x3, local copies, waits for them, and re-layouts: 2.59 us -> 0.62 us
    pallas_call x1, Pallas kernels: 74.6 us -> 73.6 us  [shards(): pl.pallas_call(kernel, out_shape=(jax.ShapeDtypeStruct((fields, levels, c...]
where the time goes in v3:
time: 77 us; the launch traced here: 76.8 us
  Pallas kernels  73.6 us (96%)
  other arithmetic  1.99 us (3%)
    pallas_call x1, Pallas kernels, shards(): pl.pallas_call(kernel, out_shape=(jax.ShapeDtypeStruct((fields, levels, c...  73.6 us
    mul x1, other arithmetic, shards(): return (2.0 * final, atm)  1.99 us

profile of v3, /device:TPU:1, one launch (start us, length us, event | category | flops | bytes accessed | tf_op | source)
XLA Modules:
  0.0 76.8 jit_solution(17372779887228471749)
XLA Ops:
  0.6 73.6 %coupled.1 = (f32[4,80,512]{2,1,0:T(8,128)}, f32[4,2048]{1,0:T(4,128)}) custom-call(f32[4,80,512]{2,1,0:T(8,128)} %ocean.1, f32[2,4,2048]{2,1,0:T(4,128)} %flux.1, f32[7,512]{1,0:T(8,128)} %coeff_in.1, s32[7,512]{1,0:T(8,128)} %near_in.1, s32[2,256]{1,0:T(2,128)} %halo_in.1, s32[1,1024]{1,0:T(1,128)} %send_in.1, s32[4,512]{1,0:T(4,128)} %slot_in.1, ...), custom_call_target="tpu_custom_call" | custom-call | tf_op jit(solution)/shard_map/coupled/pallas_call | solution.py:563
  74.2 0.0 copy-start
  74.2 2.0 %broadcast_multiply_fusion = f32[4,80,512]{2,1,0:T(8,128)} fusion(f32[4,80,512]{2,1,0:T(8,128)} %get-tuple-element.4), kind=kLoop, calls=%fused_computation | loop fusion | flops 163840 | bytes 1310720 | tf_op jit(solution)/shard_map/mul | solution.py:626
  76.2 0.0 copy-done
  76.2 0.6 copy.11
Async XLA Ops:
  74.2 2.0 %copy-start = (f32[4,2048]{1,0:T(4,128)S(1)}, f32[4,2048]{1,0:T(4,128)}, u32[]{:S(2)}) copy-start(f32[4,2048]{1,0:T(4,128)} %get-tuple-element.9) | copy-start | bytes 98308

commit v4 on v3

--- a/solution.py
+++ b/solution.py
@@ -289,6 +289,14 @@
     def push(i):
         return added[i] * profile[...]
 
+    pl.semaphore_wait(barrier, 3 * GROUP - 1)
+    for d in range(1, GROUP):
+        far = lax.rem(z + d, GROUP)
+        for n, (src, dst) in enumerate(tables):
+            remote(src, dst.at[z], table_send.at[n, far], table_recv.at[n, z], base + far).start()
+    for d in range(1, GROUP):
+        far = lax.rem(z + d, GROUP)
+        remote(ocean.at[far], state.at[z], state_send.at[far], state_recv.at[z], base + far).start()
     sums[...] = jnp.zeros_like(sums)
     level = lax.broadcasted_iota(jnp.int32, (levels, cells), 0).astype(F32)
     profile[...] = forcing_scale * jnp.exp(-level / penetration)
@@ -298,6 +306,7 @@
         [sends[:, j * LANES : (j + 1) * LANES] for j in range(PEERS)], axis=0
     )
     gather(0)
+    send_slots(0)
     for copy in own[3:]:
         copy.wait()
     step = 32
@@ -351,15 +360,6 @@
                 owner_copy(side, f, c).wait_send()
 
     at_ends(first_rims)
-    pl.semaphore_wait(barrier, 3 * GROUP - 1)
-    for d in range(1, GROUP):
-        far = lax.rem(z + d, GROUP)
-        for n, (src, dst) in enumerate(tables):
-            remote(src, dst.at[z], table_send.at[n, far], table_recv.at[n, z], base + far).start()
-    send_slots(0)
-    for d in range(1, GROUP):
-        far = lax.rem(z + d, GROUP)
-        remote(ocean.at[far], state.at[z], state_send.at[far], state_recv.at[z], base + far).start()
     at_ends(first_rims_go)
 
     def build(i):

time: 77 us -> 77.2 us (level)
  no operation moved by 1% of the time
where the time goes in v4:
time: 77.2 us; the launch traced here: 77.1 us
  Pallas kernels  73.8 us (96%)
  other arithmetic  1.99 us (3%)
    pallas_call x1, Pallas kernels, shards(): pl.pallas_call(kernel, out_shape=(jax.ShapeDtypeStruct((fields, levels, c...  73.8 us
    mul x1, other arithmetic, shards(): return (2.0 * final, atm)  1.99 us

profile of v4, /device:TPU:1, one launch (start us, length us, event | category | flops | bytes accessed | tf_op | source)
XLA Modules:
  0.0 77.1 jit_solution(10796630725872995334)
XLA Ops:
  0.6 73.8 %coupled.1 = (f32[4,80,512]{2,1,0:T(8,128)}, f32[4,2048]{1,0:T(4,128)}) custom-call(f32[4,80,512]{2,1,0:T(8,128)} %ocean.1, f32[2,4,2048]{2,1,0:T(4,128)} %flux.1, f32[7,512]{1,0:T(8,128)} %coeff_in.1, s32[7,512]{1,0:T(8,128)} %near_in.1, s32[2,256]{1,0:T(2,128)} %halo_in.1, s32[1,1024]{1,0:T(1,128)} %send_in.1, s32[4,512]{1,0:T(4,128)} %slot_in.1, ...), custom_call_target="tpu_custom_call" | custom-call | tf_op jit(solution)/shard_map/coupled/pallas_call | solution.py:563
  74.5 0.0 copy-start
  74.5 2.0 %broadcast_multiply_fusion = f32[4,80,512]{2,1,0:T(8,128)} fusion(f32[4,80,512]{2,1,0:T(8,128)} %get-tuple-element.4), kind=kLoop, calls=%fused_computation | loop fusion | flops 163840 | bytes 1310720 | tf_op jit(solution)/shard_map/mul | solution.py:626
  76.5 0.0 copy-done
  76.5 0.6 copy.11
Async XLA Ops:
  74.5 2.0 %copy-start = (f32[4,2048]{1,0:T(4,128)S(1)}, f32[4,2048]{1,0:T(4,128)}, u32[]{:S(2)}) copy-start(f32[4,2048]{1,0:T(4,128)} %get-tuple-element.9) | copy-start | bytes 98308

commit v5 on v3

--- a/solution.py
+++ b/solution.py
@@ -15,7 +15,7 @@
 STEPS = 3
 GROUP = 4
 LANES = 128
-PIECES = ((0, 48), (48, 80))
+PIECES = ((0, 80),)
 
 vertical_mix = 0.2
 forcing_scale = 0.1

time: 77 us -> 79.8 us (1.036)
  Pallas kernels: 73.6 us -> 76.4 us
    pallas_call x1, Pallas kernels: 73.6 us -> 76.4 us  [shards(): pl.pallas_call(kernel, out_shape=(jax.ShapeDtypeStruct((fields, levels, c...]
where the time goes in v5:
time: 79.8 us; the launch traced here: 79.6 us
  Pallas kernels  76.4 us (96%)
  other arithmetic  1.99 us (2%)
    pallas_call x1, Pallas kernels, shards(): pl.pallas_call(kernel, out_shape=(jax.ShapeDtypeStruct((fields, levels, c...  76.4 us
    mul x1, other arithmetic, shards(): return (2.0 * final, atm)  1.99 us

profile of v5, /device:TPU:1, one launch (start us, length us, event | category | flops | bytes accessed | tf_op | source)
XLA Modules:
  0.0 79.6 jit_solution(17017585686431202066)
XLA Ops:
  0.6 76.4 %coupled.1 = (f32[4,80,512]{2,1,0:T(8,128)}, f32[4,2048]{1,0:T(4,128)}) custom-call(f32[4,80,512]{2,1,0:T(8,128)} %ocean.1, f32[2,4,2048]{2,1,0:T(4,128)} %flux.1, f32[7,512]{1,0:T(8,128)} %coeff_in.1, s32[7,512]{1,0:T(8,128)} %near_in.1, s32[2,256]{1,0:T(2,128)} %halo_in.1, s32[1,1024]{1,0:T(1,128)} %send_in.1, s32[4,512]{1,0:T(4,128)} %slot_in.1, ...), custom_call_target="tpu_custom_call" | custom-call | tf_op jit(solution)/shard_map/coupled/pallas_call | solution.py:563
  77.0 0.0 copy-start
  77.0 2.0 %broadcast_multiply_fusion = f32[4,80,512]{2,1,0:T(8,128)} fusion(f32[4,80,512]{2,1,0:T(8,128)} %get-tuple-element.4), kind=kLoop, calls=%fused_computation | loop fusion | flops 163840 | bytes 1310720 | tf_op jit(solution)/shard_map/mul | solution.py:626
  79.0 0.0 copy-done
  79.0 0.6 copy.11
Async XLA Ops:
  77.0 2.0 %copy-start = (f32[4,2048]{1,0:T(4,128)S(1)}, f32[4,2048]{1,0:T(4,128)}, u32[]{:S(2)}) copy-start(f32[4,2048]{1,0:T(4,128)} %get-tuple-element.9) | copy-start | bytes 98308
